TPU v7x, 512 devices: a whole 4x4x16 slice. The times are simulated.
512 devices in a mesh: dp: 16 (over z_lo, y), pipe: 4 (over x), tensor: 8 (over z_hi, core).
Axes of the slice: x: 4, y: 4, z: 16 (z_hi: 4, z_lo: 4; z = z_hi * 4 + z_lo), core: 2. Of those that a mesh axis runs over, the one named last changes fastest.
Arguments:
- section_out: bfloat16 [4, 2048, 12288], P('pipe', 'dp', 'tensor'), may hold values from -6 to 6
- embedded: bfloat16 [2048, 12288], P('dp', 'tensor'), may hold values from -6 to 6
- cot_norm: bfloat16 [4, 2048, 12288], P('pipe', 'dp', 'tensor'), may hold values from -3 to 3
- cot_res: bfloat16 [4, 2048, 12288], P('pipe', 'dp', 'tensor'), may hold values from -3 to 3
- gain: bfloat16 [4, 64, 12288], P('pipe', None, 'tensor'), may hold values from 0.25 to 1.75
- bias: bfloat16 [4, 64, 12288], P('pipe', None, 'tensor'), may hold values from -1.5 to 1.5
- lang_ids: int32 [2048], P('dp'), may hold values from 0 to 63
- mb_order: int32 [16, 4], P('dp'), may hold values from 0 to 3, each once within a row
Outputs:
- normed_out: bfloat16 [4, 2048, 12288], P('pipe', 'dp', 'tensor')
- returned_grad: bfloat16 [4, 2048, 12288], P('pipe', 'dp', 'tensor')
- gain_grad: float32 [4, 64, 12288], P('pipe', None, 'tensor')
- bias_grad: float32 [4, 64, 12288], P('pipe', None, 'tensor')
Inputs may be any that keep to these rules, and one draw needn't show every extreme that they name: `lang_ids`: a language id for every token. `mb_order`: each replica's row is a permutation of the 4 micro-batches.
All inputs are finite; a program needn't handle non-finite values.
Results may differ from a plain program's by a relative error of at most 0.0004.
Values may be sent and summed in bfloat16 or wider, within the bound.
No kernel may reach another device: no remote copies, remote signals or barrier semaphores. Data moves between devices by JAX's collectives and lax.ppermute only.
A program may use at most 64 MiB of HBM per device.

v0:
```python
import jax
import jax.numpy as jnp
from jax import lax
from jax.sharding import PartitionSpec as P

D = 12288
MB = 4
eps = 1e-05


def shifted(value, axis, steps):
    count = lax.axis_size(axis)
    leading, last = (max(0, -steps), min(count, count - steps))
    return lax.ppermute(value, axis, [(source, source + steps) for source in range(leading, last)])


def passed_along(array, axis, by):
    length = lax.axis_size(axis)
    return lax.ppermute(array, axis, [(i, (i + by) % length) for i in range(length)])


def reorder(values, order):
    shaped = values.reshape((MB, -1) + values.shape[1:])
    return jnp.take(shaped, order, axis=0).reshape(values.shape)


def invert(order):
    slots = jnp.arange(MB, dtype=jnp.int32)
    hits = (order[:, None] == slots[None, :]).astype(jnp.int32)
    return jnp.sum(slots[:, None] * hits, axis=0)


def local(section_out, embedded, cot_norm, cot_res, gain, bias, lang_ids, mb_order):
    local_width = embedded.shape[1]
    langs = gain.shape[1]
    received = shifted(section_out, "pipe", 1)
    is_first = lax.axis_index("pipe") == 0
    inputs = jnp.where(is_first, embedded, received[0]).astype(jnp.float32)
    order = mb_order[0]
    inverse = invert(order)
    cot_fwd = reorder(cot_norm[0], inverse).astype(jnp.float32)
    pass_fwd = reorder(cot_res[0], inverse).astype(jnp.float32)
    matches = lang_ids[:, None] == jnp.arange(langs, dtype=jnp.int32)[None, :]
    selector = matches.astype(jnp.bfloat16)
    gain_rows = jnp.dot(selector, gain[0], preferred_element_type=jnp.float32)
    bias_rows = jnp.dot(selector, bias[0], preferred_element_type=jnp.float32)
    scaled_cot = cot_fwd * gain_rows
    moment_one, moment_two = lax.psum(
        (jnp.sum(inputs, axis=1), jnp.sum(inputs * inputs, axis=1)), "tensor"
    )
    center = moment_one[:, None] / D
    spread = moment_two[:, None] / D - center * center
    inv_scale = lax.rsqrt(spread + eps)
    normalized = (inputs - center) * inv_scale
    cot_total, cross_total = lax.psum(
        (jnp.sum(scaled_cot, axis=1), jnp.sum(scaled_cot * normalized, axis=1)), "tensor"
    )
    mean_cot = cot_total[:, None] / D
    mean_cross = cross_total[:, None] / D
    normed = (normalized * gain_rows + bias_rows).astype(jnp.bfloat16)
    input_grad = (pass_fwd + inv_scale * (scaled_cot - mean_cot - normalized * mean_cross)).astype(
        jnp.bfloat16
    )
    sent_back = reorder(input_grad, order)
    returned = passed_along(sent_back[None], "pipe", -1)
    products = jnp.concatenate([cot_fwd * normalized, cot_fwd], axis=1)
    local_sums = jnp.dot(
        matches.astype(jnp.float32).T,
        products,
        precision=lax.Precision.HIGHEST,
        preferred_element_type=jnp.float32,
    )
    summed = lax.psum(local_sums, "dp")
    return (normed[None], returned, summed[:, :local_width][None], summed[:, local_width:][None])


def solution(mesh):
    return jax.shard_map(
        local,
        mesh=mesh,
        in_specs=(
            P("pipe", "dp", "tensor"),
            P("dp", "tensor"),
            P("pipe", "dp", "tensor"),
            P("pipe", "dp", "tensor"),
            P("pipe", None, "tensor"),
            P("pipe", None, "tensor"),
            P("dp"),
            P("dp", None),
        ),
        out_specs=(
            P("pipe", "dp", "tensor"),
            P("pipe", "dp", "tensor"),
            P("pipe", None, "tensor"),
            P("pipe", None, "tensor"),
        ),
        check_vma=False,
    )
```

profile of v0, /device:TPU:2, one launch (start us, length us, event | category | flops | bytes accessed | tf_op | source)
XLA Modules:
  0.0 227.5 jit_solution(1984460876628142965)
XLA Ops:
  7.2 0.0 all-reduce.4.cloned.1.call-start
  7.2 3.5 %collective-permute-start = (bf16[1,128,1536]{2,1,0:T(8,128)(2,1)}, bf16[1,128,1536]{2,1,0:T(8,128)(2,1)S(1)}, u32[]{:S(2)}, u32[]{:S(2)}) collective-permute-start(bf16[1,128,1536]{2,1,0:T(8,128)(2,1)} %param.10), channel_id=1, source_target_pairs={{0,8},{8,16},{16,24},{1,9},{9,17},{17,25},{2,10},{10,18},{18,26},{... | collective-permute-start | bytes 1179656 | tf_op jit(solution)/shard_map/ppermute | solution.py:14
  10.8 0.7 select_reduce_fusion
  11.5 0.7 compare_select_fusion
  12.2 0.7 compare_and_fusion
  12.9 0.6 gather_fusion
  13.5 0.6 gather_fusion.1
  14.1 0.1 broadcast_select_fusion.1
  14.2 0.1 bitcast_convert_fusion
  14.3 6.2 %collective-permute-done = bf16[1,128,1536]{2,1,0:T(8,128)(2,1)S(1)} collective-permute-done((bf16[1,128,1536]{2,1,0:T(8,128)(2,1)}, bf16[1,128,1536]{2,1,0:T(8,128)(2,1)S(1)}, u32[]{:S(2)}, u32[]{:S(2)}) %collective-permute-start) | collective-permute-done | bytes 393248 | tf_op jit(solution)/shard_map/ppermute | solution.py:14
  20.5 0.2 convert_reduce_fusion
  20.8 27.0 %all-reduce.1 = (f32[128]{0:T(128)S(1)}, f32[128]{0:T(128)S(1)}) all-reduce(f32[128]{0:T(128)S(1)} %get-tuple-element.8, f32[128]{0:T(128)S(1)} %get-tuple-element.7), channel_id=1, replica_groups=mesh['dp'=16,'pipe'=4,'tensor'=8] {'tensor'}, use_global_device_ids=true, to_apply=%region_3.4 | all-reduce | flops 256 | bytes 2048 | tf_op jit(solution)/shard_map/psum | solution.py:48
  47.8 0.5 fusion.17
  48.3 1.7 fusion.2
  50.0 18.8 %all-reduce = (f32[128]{0:T(128)S(1)}, f32[128]{0:T(128)S(1)}) all-reduce(f32[128]{0:T(128)S(1)} %get-tuple-element.6, f32[128]{0:T(128)S(1)} %get-tuple-element.5), channel_id=1, replica_groups=mesh['dp'=16,'pipe'=4,'tensor'=8] {'tensor'}, use_global_device_ids=true, to_apply=%region_8.10 | all-reduce | flops 256 | bytes 2048 | tf_op jit(solution)/shard_map/psum | solution.py:55
  68.8 0.4 fusion.15
  69.1 0.6 gather_fusion.2
  69.7 0.1 broadcast_select_fusion
  69.8 1.9 collective-permute-start.1
  71.8 1.1 fusion.1
  72.8 8.8 %collective-permute-done.1 = bf16[1,128,1536]{2,1,0:T(8,128)(2,1)S(1)} collective-permute-done((bf16[1,128,1536]{2,1,0:T(8,128)(2,1)S(1)}, bf16[1,128,1536]{2,1,0:T(8,128)(2,1)S(1)}, u32[]{:S(2)}, u32[]{:S(2)}) %collective-permute-start.1) | collective-permute-done | bytes 393248 | tf_op jit(solution)/shard_map/ppermute | solution.py:19
  81.7 136.2 %all-reduce.4.cloned.1.call-done = f32[64,3072]{1,0:T(8,128)} async-done(((f32[64,3072]{1,0:T(8,128)}), f32[64,3072]{1,0:T(8,128)}) %all-reduce.4.cloned.1.call-update) | async-done | bytes 786448 | tf_op jit(solution)/shard_map/psum | solution.py:73
  217.9 2.0 slice_bitcast_fusion
  220.0 0.7 copy.14
  (19 shorter events, 0.1 us)
Async XLA Ops:
  7.2 5.7 %copy-start = (bf16[1,128,1536]{2,1,0:T(8,128)(2,1)S(1)}, bf16[1,128,1536]{2,1,0:T(8,128)(2,1)}, u32[]{:S(2)}) copy-start(bf16[1,128,1536]{2,1,0:T(8,128)(2,1)} %param.13) | copy-start | bytes 1179652
  7.2 6.3 %copy-start.2 = (bf16[1,128,1536]{2,1,0:T(8,128)(2,1)S(1)}, bf16[1,128,1536]{2,1,0:T(8,128)(2,1)}, u32[]{:S(2)}) copy-start(bf16[1,128,1536]{2,1,0:T(8,128)(2,1)} %param.12) | copy-start | bytes 1179652
  7.2 210.7 %all-reduce.4.cloned.1.call-start = ((), (), s32[]{:S(2)}) async-start(), calls=%async_computation | async-start | bytes 1572864 | tf_op jit(solution)/shard_map/psum | solution.py:73
  7.2 13.3 %collective-permute-start = (bf16[1,128,1536]{2,1,0:T(8,128)(2,1)}, bf16[1,128,1536]{2,1,0:T(8,128)(2,1)S(1)}, u32[]{:S(2)}, u32[]{:S(2)}) collective-permute-start(bf16[1,128,1536]{2,1,0:T(8,128)(2,1)} %param.10), channel_id=1, source_target_pairs={{0,8},{8,16},{16,24},{1,9},{9,17},{17,25},{2,10},{10,18},{18,26},{... | collective-permute-start | bytes 1179656 | tf_op jit(solution)/shard_map/ppermute | solution.py:14
  14.2 6.3 %copy-start.1 = (bf16[128,1536]{1,0:T(8,128)(2,1)S(1)}, bf16[128,1536]{1,0:T(8,128)(2,1)}, u32[]{:S(2)}) copy-start(bf16[128,1536]{1,0:T(8,128)(2,1)} %param.11) | copy-start | bytes 1179652
  14.3 33.5 %copy-start.3 = (bf16[1,64,1536]{2,1,0:T(8,128)(2,1)S(1)}, bf16[1,64,1536]{2,1,0:T(8,128)(2,1)}, u32[]{:S(2)}) copy-start(bf16[1,64,1536]{2,1,0:T(8,128)(2,1)} %param.14) | copy-start | bytes 589828
  14.3 33.5 %copy-start.5 = (s32[128]{0:T(128)S(1)}, s32[128]{0:T(128)}, u32[]{:S(2)}) copy-start(s32[128]{0:T(128)} %param.16) | copy-start | bytes 1540
  69.1 2.6 %copy-start.4 = (bf16[1,64,1536]{2,1,0:T(8,128)(2,1)S(1)}, bf16[1,64,1536]{2,1,0:T(8,128)(2,1)}, u32[]{:S(2)}) copy-start(bf16[1,64,1536]{2,1,0:T(8,128)(2,1)} %param.15) | copy-start | bytes 589828
  69.8 11.8 %collective-permute-start.1 = (bf16[1,128,1536]{2,1,0:T(8,128)(2,1)S(1)}, bf16[1,128,1536]{2,1,0:T(8,128)(2,1)S(1)}, u32[]{:S(2)}, u32[]{:S(2)}) collective-permute-start(bf16[1,128,1536]{2,1,0:T(8,128)(2,1)S(1)} %bitcast.42), channel_id=1, source_target_pairs={{0,24},{8,0},{16,8},{24,16},{1,25},{9,1},{17,9},{25,17},{2,26},{10... | collective-permute-start | bytes 1179656 | tf_op jit(solution)/shard_map/ppermute | solution.py:19
Sparse Core Ops, SparseCore 0:
  50.1 167.7 all-reduce.3
where the time goes:
time: 228 us
  waiting for transfers between devices  151 us (66%)
  blocking collectives  45.8 us (20%)
  between operations  14.2 us (6%)
  starting transfers between devices  5.49 us (2%)
  local copies, waits for them, and re-layouts  4.55 us (2%)
  matrix products  3.23 us (1%)
  other arithmetic  3.06 us (1%)
    psum x1, waiting for transfers between devices, local(): summed = lax.psum(local_sums, 'dp')  136 us
    psum x1, blocking collectives, local(): lax.psum((jnp.sum(inputs, axis=1), jnp.sum(inputs * inputs, axis=1)), 'te...  27 us
    psum x1, blocking collectives, local(): lax.psum((jnp.sum(scaled_cot, axis=1), jnp.sum(scaled_cot * normalized, a...  18.8 us
    ppermute x1, waiting for transfers between devices, passed_along(): lax.ppermute(array, axis, [(i, (i + by) % length) for i in range(length)])  8.85 us
    ppermute x1, waiting for transfers between devices, shifted(): lax.ppermute(value, axis, [(source, source + steps) for source in range(l...  6.17 us
  transfers between devices with their start and end apart: 3, of which 3 were waited for; matrix products, arithmetic and copies ran while one was open for 2% of the time, Pallas kernels for 0%

commit v1 on v0

--- a/solution.py
+++ b/solution.py
@@ -70,7 +70,7 @@
         precision=lax.Precision.HIGHEST,
         preferred_element_type=jnp.float32,
     )
-    summed = lax.psum(local_sums, "dp")
+    summed = jnp.sum(lax.all_gather(local_sums, "dp"), axis=0)
     return (normed[None], returned, summed[:, :local_width][None], summed[:, local_width:][None])
 
 

time: 228 us -> 211 us (0.925)
  the two profiles are of different devices: /device:TPU:2 before, /device:TPU:1 now
where the time goes in v1:
time: 211 us
  waiting for transfers between devices  122 us (58%)
  blocking collectives  49 us (23%)
  between operations  14.2 us (7%)
  starting transfers between devices  10.2 us (5%)
  other arithmetic  8.14 us (4%)
  local copies, waits for them, and re-layouts  4.43 us (2%)
  matrix products  3.24 us (2%)
    all_gather x1, waiting for transfers between devices, local(): summed = jnp.sum(lax.all_gather(local_sums, 'dp'), axis=0)  115 us
    psum x1, blocking collectives, local(): lax.psum((jnp.sum(inputs, axis=1), jnp.sum(inputs * inputs, axis=1)), 'te...  27.1 us
    psum x1, blocking collectives, local(): lax.psum((jnp.sum(scaled_cot, axis=1), jnp.sum(scaled_cot * normalized, a...  21.9 us
    ppermute x1, waiting for transfers between devices, passed_along(): lax.ppermute(array, axis, [(i, (i + by) % length) for i in range(length)])  5.69 us
    reduce_sum x1, other arithmetic, local(): summed = jnp.sum(lax.all_gather(local_sums, 'dp'), axis=0)  5.39 us
    ppermute x1, starting transfers between devices, passed_along(): lax.ppermute(array, axis, [(i, (i + by) % length) for i in range(length)])  5.37 us
    ppermute x1, starting transfers between devices, shifted(): lax.ppermute(value, axis, [(source, source + steps) for source in range(l...  4.82 us
  transfers between devices with their start and end apart: 3, of which 3 were waited for; matrix products, arithmetic and copies ran while one was open for 2% of the time, Pallas kernels for 0%

profile of v1, /device:TPU:1, one launch (start us, length us, event | category | flops | bytes accessed | tf_op | source)
XLA Modules:
  0.0 210.9 jit_solution(11721272389914477621)
XLA Ops:
  7.2 0.0 all-gather.3.cloned.1.call-start
  7.2 4.8 %collective-permute-start = (bf16[1,128,1536]{2,1,0:T(8,128)(2,1)}, bf16[1,128,1536]{2,1,0:T(8,128)(2,1)}, u32[]{:S(2)}, u32[]{:S(2)}) collective-permute-start(bf16[1,128,1536]{2,1,0:T(8,128)(2,1)} %param.10), channel_id=1, source_target_pairs={{0,8},{8,16},{16,24},{1,9},{9,17},{17,25},{2,10},{10,18},{18,26},{... | collective-permute-start | bytes 1179656 | tf_op jit(solution)/shard_map/ppermute | solution.py:14
  12.0 0.7 select_reduce_fusion
  12.8 0.6 gather_fusion.1
  13.4 1.6 gather_fusion
  15.0 0.1 broadcast_select_fusion.1
  15.2 0.1 bitcast_convert_fusion
  15.3 1.1 collective-permute-done
  16.3 1.2 convert_reduce_fusion
  17.6 27.1 %all-reduce.1 = (f32[128]{0:T(128)S(1)}, f32[128]{0:T(128)S(1)}) all-reduce(f32[128]{0:T(128)S(1)} %get-tuple-element.8, f32[128]{0:T(128)S(1)} %get-tuple-element.7), channel_id=1, replica_groups=mesh['dp'=16,'pipe'=4,'tensor'=8] {'tensor'}, use_global_device_ids=true, to_apply=%region_3.4 | all-reduce | flops 256 | bytes 2048 | tf_op jit(solution)/shard_map/psum | solution.py:48
  44.7 0.5 fusion.17
  45.2 1.7 fusion.2
  46.9 0.0 all-gather.3.cloned.1.call-update
  46.9 21.9 %all-reduce = (f32[128]{0:T(128)S(1)}, f32[128]{0:T(128)S(1)}) all-reduce(f32[128]{0:T(128)S(1)} %get-tuple-element.6, f32[128]{0:T(128)S(1)} %get-tuple-element.5), channel_id=1, replica_groups=mesh['dp'=16,'pipe'=4,'tensor'=8] {'tensor'}, use_global_device_ids=true, to_apply=%region_8.10 | all-reduce | flops 256 | bytes 2048 | tf_op jit(solution)/shard_map/psum | solution.py:55
  68.9 0.4 fusion.15
  69.2 0.6 gather_fusion.2
  69.8 0.1 broadcast_select_fusion
  69.9 5.4 %collective-permute-start.1 = (bf16[1,128,1536]{2,1,0:T(8,128)(2,1)S(1)}, bf16[1,128,1536]{2,1,0:T(8,128)(2,1)S(1)}, u32[]{:S(2)}, u32[]{:S(2)}) collective-permute-start(bf16[1,128,1536]{2,1,0:T(8,128)(2,1)S(1)} %bitcast.44), channel_id=1, source_target_pairs={{0,24},{8,0},{16,8},{24,16},{1,25},{9,1},{17,9},{25,17},{2,26},{10... | collective-permute-start | bytes 1179656 | tf_op jit(solution)/shard_map/ppermute | solution.py:19
  75.3 1.1 fusion.1
  76.4 5.7 %collective-permute-done.1 = bf16[1,128,1536]{2,1,0:T(8,128)(2,1)S(1)} collective-permute-done((bf16[1,128,1536]{2,1,0:T(8,128)(2,1)S(1)}, bf16[1,128,1536]{2,1,0:T(8,128)(2,1)S(1)}, u32[]{:S(2)}, u32[]{:S(2)}) %collective-permute-start.1) | collective-permute-done | bytes 393248 | tf_op jit(solution)/shard_map/ppermute | solution.py:19
  82.0 114.9 %all-gather.3.cloned.1.call-done = f32[1024,3072]{1,0:T(8,128)} async-done(((f32[64,3072]{1,0:T(8,128)}), f32[1024,3072]{1,0:T(8,128)}) %all-gather.3.cloned.1.call-update) | async-done | bytes 12582928 | tf_op jit(solution)/shard_map/all_gather | solution.py:73
  196.9 5.4 %reduce_sum.59 = f32[64,3072]{1,0:T(8,128)S(1)} reduce(f32[16,64,3072]{2,1,0:T(8,128)} %bitcast.41, f32[]{:T(128)} %constant.25.clone.1), dimensions={0}, to_apply=%region_9.11 | reduce | flops 2949120 | bytes 13369348 | tf_op jit(solution)/shard_map/reduce_sum | solution.py:73
  202.3 0.9 slice_bitcast_fusion
  203.3 0.7 copy.13
  (20 shorter events, 0.1 us)
Async XLA Ops:
  7.2 5.7 %copy-start = (bf16[1,128,1536]{2,1,0:T(8,128)(2,1)S(1)}, bf16[1,128,1536]{2,1,0:T(8,128)(2,1)}, u32[]{:S(2)}) copy-start(bf16[1,128,1536]{2,1,0:T(8,128)(2,1)} %param.12) | copy-start | bytes 1179652
  7.2 189.8 %all-gather.3.cloned.1.call-start = ((), (), s32[]{:S(2)}) async-start(), calls=%async_computation | async-start | bytes 13369344 | tf_op jit(solution)/shard_map/all_gather | solution.py:73
  7.2 9.1 %collective-permute-start = (bf16[1,128,1536]{2,1,0:T(8,128)(2,1)}, bf16[1,128,1536]{2,1,0:T(8,128)(2,1)}, u32[]{:S(2)}, u32[]{:S(2)}) collective-permute-start(bf16[1,128,1536]{2,1,0:T(8,128)(2,1)} %param.10), channel_id=1, source_target_pairs={{0,8},{8,16},{16,24},{1,9},{9,17},{17,25},{2,10},{10,18},{18,26},{... | collective-permute-start | bytes 1179656 | tf_op jit(solution)/shard_map/ppermute | solution.py:14
  15.0 1.3 copy-start.1
  15.1 29.5 %copy-start.2 = (bf16[1,64,1536]{2,1,0:T(8,128)(2,1)S(1)}, bf16[1,64,1536]{2,1,0:T(8,128)(2,1)}, u32[]{:S(2)}) copy-start(bf16[1,64,1536]{2,1,0:T(8,128)(2,1)} %param.14) | copy-start | bytes 589828
  15.2 29.5 %copy-start.4 = (s32[128]{0:T(128)S(1)}, s32[128]{0:T(128)}, u32[]{:S(2)}) copy-start(s32[128]{0:T(128)} %param.16) | copy-start | bytes 1540
  45.2 1.7 copy-start.5
  68.9 6.4 %copy-start.3 = (bf16[1,64,1536]{2,1,0:T(8,128)(2,1)S(1)}, bf16[1,64,1536]{2,1,0:T(8,128)(2,1)}, u32[]{:S(2)}) copy-start(bf16[1,64,1536]{2,1,0:T(8,128)(2,1)} %param.15) | copy-start | bytes 589828
  69.9 12.1 %collective-permute-start.1 = (bf16[1,128,1536]{2,1,0:T(8,128)(2,1)S(1)}, bf16[1,128,1536]{2,1,0:T(8,128)(2,1)S(1)}, u32[]{:S(2)}, u32[]{:S(2)}) collective-permute-start(bf16[1,128,1536]{2,1,0:T(8,128)(2,1)S(1)} %bitcast.44), channel_id=1, source_target_pairs={{0,24},{8,0},{16,8},{24,16},{1,25},{9,1},{17,9},{25,17},{2,26},{10... | collective-permute-start | bytes 1179656 | tf_op jit(solution)/shard_map/ppermute | solution.py:19
Sparse Core Ops, SparseCore 0:
  47.0 149.8 all-gather.2
